TPU v7x, 256 devices: a whole 4x4x8 slice. The times are simulated.
256 devices in a mesh: ctx: 32 (over z, y_hi, core), head: 8 (over x, y_lo).
Axes of the slice: x: 4, y: 4 (y_hi: 2, y_lo: 2; y = y_hi * 2 + y_lo), z: 8, core: 2. Of those that a mesh axis runs over, the one named last changes fastest.
Arguments:
- response_input: bfloat16 [512, 8192], P(('ctx', 'head')), may hold values from -6 to 6
- response_queries: bfloat16 [512, 8192], P(('ctx', 'head')), may hold values from -12 to 12
- response_keys: bfloat16 [512, 8192], P(('ctx', 'head')), may hold values from -6 to 6
- response_values: bfloat16 [512, 8192], P(('ctx', 'head')), may hold values from -6 to 6
- prompt_keys: bfloat16 [49152, 8192], P('ctx', 'head'), may hold values from -6 to 6
- prompt_values: bfloat16 [49152, 8192], P('ctx', 'head'), may hold values from -6 to 6
- query_down_weight: bfloat16 [8192, 16], replicated, may hold values from -0.0625 to 0.0625
- query_up_weight: bfloat16 [16, 8192], replicated, may hold values from -1.5 to 1.5
- value_down_weight: bfloat16 [8192, 16], replicated, may hold values from -0.0625 to 0.0625
- value_up_weight: bfloat16 [16, 8192], replicated, may hold values from -1.5 to 1.5
- response_index: int32 [512], replicated, may hold values from 0 to 7, never falling along the last dimension, each value on 1 to 128 neighbouring positions
Outputs:
- out_adapted: bfloat16 [512, 8192], P(('ctx', 'head'))
- out_base: bfloat16 [512, 8192], P(('ctx', 'head'))
Inputs may be any that keep to these rules, and one draw needn't show every extreme that they name: `response_index`: never falls along the tokens; each response spans 1 to 128 tokens and one spans exactly 128.
All inputs are finite; a program needn't handle non-finite values.
Results may differ from a plain program's by a relative error of at most 0.0088.
Values may be sent and summed in bfloat16 or wider, within the bound.
No kernel may reach another device: no remote copies, remote signals or barrier semaphores. Data moves between devices by JAX's collectives and lax.ppermute only.
A program may use at most 64 MiB of HBM per device.

v0:
```python
import jax
import jax.numpy as jnp
from jax import lax
from jax.experimental import pallas as pl
from jax.experimental.pallas import tpu as pltpu
from jax.sharding import Mesh, PartitionSpec as P


HD = 128
SCALE = HD**-0.5
LOG2E = 1.4426950408889634
HIDDEN = -1e30
KEY_CHUNK = 256
LAST_DIMS = (((1,), (1,)), ((), ()))
BF16 = jnp.bfloat16
F32 = jnp.float32


def swap(size, flip=1):
    return [(i, i ^ flip) for i in range(size)]


VMEM = pl.BlockSpec(memory_space=pltpu.VMEM)
HBM = pl.BlockSpec(memory_space=pltpu.HBM)


def small(limit=12):
    return pltpu.CompilerParams(vmem_limit_bytes=limit << 20)


def prepare_kernel(x_ref, q_ref, k_ref, v_ref, wq_ref, wv_ref, out_ref, f_ref):
    rank = wq_ref.shape[0]
    x = x_ref[...]
    f_ref[...] = jnp.zeros_like(f_ref)
    f_ref[0, :, :rank] = lax.dot_general(x, wq_ref[...], LAST_DIMS, preferred_element_type=F32)
    f_ref[1, :, :rank] = lax.dot_general(x, wv_ref[...], LAST_DIMS, preferred_element_type=F32)
    fq = f_ref[0].astype(BF16)
    fv = f_ref[1].astype(BF16)
    for g in range(q_ref.shape[0]):
        at = 0
        for piece in (q_ref[g], fq, k_ref[g], v_ref[g], fv):
            out_ref[g, :, at : at + piece.shape[1]] = piece
            at += piece.shape[1]


def prepare(x, q, k, v, wq, wv):
    groups, rows, width = q.shape
    return pl.pallas_call(
        prepare_kernel,
        out_shape=jax.ShapeDtypeStruct((groups, rows, 3 * width + 256), BF16),
        scratch_shapes=[pltpu.VMEM((2, rows, 128), F32)],
        name="prepare",
    )(x, q, k, v, wq, wv)


def fan_kernel(near_ref, far_ref, out_ref):
    rows, padded = far_ref.shape
    near = near_ref[:, :padded]
    far = far_ref[...]
    for z in range(out_ref.shape[0]):
        out_ref[z, :rows] = near
        out_ref[z, rows:] = far


def fan(near, far, parts):
    rows, padded = far.shape
    return pl.pallas_call(
        fan_kernel,
        out_shape=jax.ShapeDtypeStruct((parts, 2 * rows, padded), BF16),
        name="fan",
    )(near, far)


def pack_lse(lse, lane):
    lse = jnp.where(lane < 8, lse, 0.0)
    high = lse.astype(BF16).astype(F32)
    middle = (lse - high).astype(BF16).astype(F32)
    low = lse - high - middle
    return (high + pltpu.roll(middle, 8, 1) + pltpu.roll(low, 16, 1)).astype(BF16)


def unpack_lse(packed):
    x = packed.astype(F32)
    return x + pltpu.roll(x, 120, 1) + pltpu.roll(x, 112, 1)


def attend_kernel(
    where_ref, own_ref, other_ref, keys_hbm, values_hbm, stretch_ref, wq_ref, wv_ref, bias_ref, after_ref,
    own_out_ref, other_out_ref, keys_ref, values_ref, s0_ref, s1_ref, m0_ref, m1_ref, o_ref, l_ref, sems,
):
    del after_ref
    side = where_ref[0]
    shards, _, shard_rows, _ = own_ref.shape
    n = shards * shard_rows
    rows = 4 * n
    kn, width = keys_ref.shape
    heads = width // HD
    rank = wq_ref.shape[0]
    scores_refs = (s0_ref, s1_ref)
    max_refs = (m0_ref, m1_ref)
    lane = lax.broadcasted_iota(jnp.int32, (n, 128), 1)
    bias_own = bias_ref[where_ref[1]]
    bias_other = bias_ref[where_ref[2]]
    keys_at = width + 128
    values_at = keys_at + width
    factors_at = values_at + width
    bias = jnp.concatenate([bias_own, bias_other, bias_own, bias_other], 0)

    def fetch(i, h):
        src, dst = ((keys_hbm, keys_ref), (values_hbm, values_ref))[i]
        cols = slice(h * HD, (h + 1) * HD)
        return pltpu.make_async_copy(src.at[:, cols], dst.at[:, cols], sems.at[i, h])

    order = [(0, 0), (0, 1), (1, 0)] + [(i, h) for h in range(1, heads) for i, h in ((0, h + 1), (1, h)) if h < heads]
    for i, h in order:
        fetch(i, h).start()

    def tokens(ref, at, size):
        return ref[:, side, :, at : at + size].reshape(n, size)

    factors = jnp.concatenate([tokens(own_ref, width, HD), tokens(other_ref, width, HD)], 0)[:, :rank]
    value_factors = stretch_ref[:, factors_at : factors_at + rank]

    def begin(h):
        at = h * HD
        base = jnp.concatenate([tokens(own_ref, at, HD), tokens(other_ref, at, HD)], 0)
        adapted = (
            base.astype(F32) + jnp.dot(factors, wq_ref[:, at : at + HD], preferred_element_type=F32)
        ).astype(BF16)
        q = jnp.concatenate([adapted, base], 0)
        near = lax.dot_general(q, stretch_ref[:, keys_at + at : keys_at + at + HD], LAST_DIMS, preferred_element_type=F32) + bias
        max_refs[h % 2][...] = jnp.broadcast_to(jnp.max(near, -1, keepdims=True), (rows, 128))
        return q, near

    def score(h, q, j):
        s = lax.dot_general(
            q, keys_ref[j : j + KEY_CHUNK, h * HD : (h + 1) * HD], LAST_DIMS, preferred_element_type=F32
        )
        scores_refs[h % 2][:, j : j + KEY_CHUNK] = s
        m = max_refs[h % 2][...]
        for c in range(0, KEY_CHUNK, 128):
            m = jnp.maximum(m, s[:, c : c + 128])
        max_refs[h % 2][...] = m

    q, near = begin(0)
    fetch(0, 0).wait()
    for j in range(0, kn, KEY_CHUNK):
        score(0, q, j)
    fetch(0, 1).wait()
    fetch(1, 0).wait()
    lses = [jnp.zeros((n, 128), F32) for _ in range(4)]
    for h in range(heads):
        at = h * HD
        if h + 1 < heads:
            q, near_next = begin(h + 1)
        m = jnp.max(max_refs[h % 2][...], -1, keepdims=True)
        shift = m * (SCALE * LOG2E)
        near_probs = jnp.exp2(near * (SCALE * LOG2E) - shift)
        near_total = jnp.sum(near_probs, -1, keepdims=True)
        near_probs = near_probs.astype(BF16)
        base_values = stretch_ref[:, values_at + at : values_at + at + HD]
        adapted_values = (
            base_values.astype(F32) + jnp.dot(value_factors, wv_ref[:, at : at + HD], preferred_element_type=F32)
        ).astype(BF16)
        o_ref[: 2 * n] = jnp.dot(near_probs[: 2 * n], adapted_values, preferred_element_type=F32)
        o_ref[2 * n :] = jnp.dot(near_probs[2 * n :], base_values, preferred_element_type=F32)
        l_ref[...] = jnp.zeros_like(l_ref)
        for j in range(0, kn, KEY_CHUNK):
            if h + 1 < heads:
                score(h + 1, q, j)
            p = jnp.exp2(scores_refs[h % 2][:, j : j + KEY_CHUNK] * (SCALE * LOG2E) - shift)
            total = l_ref[...]
            for c in range(0, KEY_CHUNK, 128):
                total += p[:, c : c + 128]
            l_ref[...] = total
            o_ref[...] += jnp.dot(
                p.astype(BF16), values_ref[j : j + KEY_CHUNK, at : at + HD], preferred_element_type=F32
            )
        total = jnp.sum(l_ref[...], -1, keepdims=True) + near_total
        mean = (o_ref[...] / total).astype(BF16)
        lse = m * SCALE + jnp.log(total)
        for stream in range(2):
            for partner, out_ref in enumerate((own_out_ref, other_out_ref)):
                i = 2 * stream + partner
                out_ref[stream, :, at : at + HD] = mean[i * n : (i + 1) * n]
                lses[i] = jnp.where(lane == h, lse[i * n : (i + 1) * n], lses[i])
        if h + 1 < heads:
            near = near_next
        if h == 0:
            for i, later in order[3:]:
                fetch(i, later).wait()
    for stream in range(2):
        own_out_ref[stream, :, width:] = pack_lse(lses[2 * stream], lane)
        other_out_ref[stream, :, width:] = pack_lse(lses[2 * stream + 1], lane)


def attend(where, own, other, keys, values, stretch, wq, wv, bias, after):
    shards, _, shard_rows, padded = own.shape
    n = shards * shard_rows
    kn, width = keys.shape
    heads = width // HD
    out = jax.ShapeDtypeStruct((2, n, padded), BF16)
    return pl.pallas_call(
        attend_kernel,
        in_specs=[pl.BlockSpec(memory_space=pltpu.SMEM), VMEM, VMEM, HBM, HBM] + [VMEM] * 4 + [HBM],
        out_specs=[VMEM, VMEM],
        out_shape=[out, out],
        scratch_shapes=[pltpu.VMEM((kn, width), BF16)] * 2
        + [pltpu.VMEM((4 * n, kn), F32)] * 2
        + [pltpu.VMEM((4 * n, 128), F32)] * 4
        + [pltpu.SemaphoreType.DMA((2, heads))],
        cost_estimate=pl.CostEstimate(
            flops=16 * n * kn * heads * HD, bytes_accessed=4 * kn * width, transcendentals=4 * n * kn * heads
        ),
        compiler_params=small(51),
        name="attend",
    )(where, own, other, keys, values, stretch, wq, wv, bias, after)


def merge(pieces, width):
    lane = lax.broadcasted_iota(jnp.int32, (pieces[0].shape[0], 128), 1)
    lses = [unpack_lse(x[:, width:]) for x in pieces]
    best = lses[0]
    for lse in lses[1:]:
        best = jnp.maximum(best, lse)
    weights = [jnp.exp(lse - best) for lse in lses]
    total = weights[0]
    for w in weights[1:]:
        total = total + w
    weights = [w / total for w in weights]
    means = []
    for h in range(width // HD):
        at = h * HD
        mean = weights[0][:, h : h + 1] * pieces[0][:, at : at + HD].astype(F32)
        for w, x in zip(weights[1:], pieces[1:]):
            mean += w[:, h : h + 1] * x[:, at : at + HD].astype(F32)
        means.append(mean.astype(BF16))
    return means, pack_lse(best + jnp.log(total), lane)


def merge_pair_kernel(a_ref, b_ref, out_ref):
    width = out_ref.shape[2] - 128
    for s in range(2):
        means, lse = merge([a_ref[s], b_ref[s]], width)
        for h, mean in enumerate(means):
            out_ref[s, :, h * HD : (h + 1) * HD] = mean
        out_ref[s, :, width:] = lse


def merge_pair(a, b):
    return pl.pallas_call(
        merge_pair_kernel,
        in_specs=[VMEM, VMEM],
        out_specs=VMEM,
        compiler_params=small(),
        out_shape=jax.ShapeDtypeStruct(a.shape, BF16),
        cost_estimate=pl.CostEstimate(flops=8 * a.size, bytes_accessed=6 * a.size, transcendentals=0),
        name="merge_pair",
    )(a, b)


def merge_send_kernel(a_ref, b_ref, c_ref, out_ref):
    width = out_ref.shape[3] - 128
    for s in range(2):
        means, lse = merge([a_ref[s], b_ref[s], c_ref[s]], width)
        for at, block in enumerate(means + [lse]):
            for p in range(out_ref.shape[0]):
                out_ref[p, s, :, at * HD : (at + 1) * HD] = block[2 * p : 2 * p + 2]


def merge_send(a, b, c):
    _, n, padded = a.shape
    return pl.pallas_call(
        merge_send_kernel,
        in_specs=[VMEM, VMEM, VMEM],
        out_specs=VMEM,
        compiler_params=small(),
        out_shape=jax.ShapeDtypeStruct((n // 2, 2, 2, padded), BF16),
        cost_estimate=pl.CostEstimate(flops=12 * a.size, bytes_accessed=8 * a.size, transcendentals=0),
        name="merge_send",
    )(a, b, c)


def finish_kernel(x_ref, a_ref, b_ref):
    parts = x_ref.shape[0]
    groups, rows, width = a_ref.shape
    means, _ = merge([x_ref[z] for z in range(parts)], width)
    for h, mean in enumerate(means):
        for g in range(groups):
            at = 2 * rows * g
            a_ref[g, :, h * HD : (h + 1) * HD] = mean[at : at + rows]
            b_ref[g, :, h * HD : (h + 1) * HD] = mean[at + rows : at + 2 * rows]


def finish(x, groups, rows):
    out = jax.ShapeDtypeStruct((groups, rows, x.shape[2] - 128), BF16)
    return pl.pallas_call(
        finish_kernel, in_specs=[VMEM], out_specs=[VMEM, VMEM], out_shape=(out, out), compiler_params=small(), name="finish"
    )(x)


def local(
    response_input,
    response_queries,
    response_keys,
    response_values,
    prompt_keys,
    prompt_values,
    query_down_weight,
    query_up_weight,
    value_down_weight,
    value_up_weight,
    response_index,
):
    nz, ny, nc = (lax.axis_size(a) for a in ("z", "yh", "c"))
    groups = lax.axis_size("x") * lax.axis_size("yl")
    rows, model = response_queries.shape
    width = model // groups
    shard_rows = rows * groups
    side, core = lax.axis_index("yh"), lax.axis_index("c")
    part = (lax.axis_index("z") * ny + side) * nc + core
    group = lax.axis_index("x") * lax.axis_size("yl") + lax.axis_index("yl")

    def by_group(a):
        return a.reshape(rows, groups, width).transpose(1, 0, 2)

    padded = width + 128
    sent = prepare(
        response_input,
        by_group(response_queries),
        by_group(response_keys),
        by_group(response_values),
        query_down_weight.T,
        value_down_weight.T,
    )
    stretch = lax.all_to_all(sent, ("x", "yl"), 0, 0, tiled=True).reshape(shard_rows, 3 * width + 256)
    far_rows = lax.ppermute(stretch[:, :padded], "yh", swap(ny))
    own = lax.all_to_all(fan(stretch, far_rows, nz), "z", 0, 0, tiled=True)
    other = lax.ppermute(own, "c", swap(nc))
    own = own.reshape(nz, ny, shard_rows, padded)
    other = other.reshape(nz, ny, shard_rows, padded)

    wq = lax.dynamic_slice_in_dim(query_up_weight, group * width, width, 1)
    wv = lax.dynamic_slice_in_dim(value_up_weight, group * width, width, 1)
    count = response_index.shape[0]
    key_pos = part * shard_rows + jnp.arange(shard_rows, dtype=jnp.int32)
    key_seg = lax.dynamic_slice_in_dim(response_index, part * shard_rows, shard_rows, 0)
    query_pos = jnp.arange(count, dtype=jnp.int32)
    seen = (key_pos[None, :] <= query_pos[:, None]) & (key_seg[None, :] == response_index[:, None])
    bias = jnp.where(seen, 0.0, HIDDEN).astype(F32)
    bias = bias.reshape(nz, ny * nc, shard_rows, shard_rows).transpose(1, 0, 2, 3)
    bias = bias.reshape(ny * nc, nz * shard_rows, shard_rows)

    def attend_side(far, after):
        half = 2 * (side ^ far)
        where = jnp.stack([jnp.int32(far), half + core, half + 1 - core]).astype(jnp.int32)
        return attend(where, own, other, prompt_keys, prompt_values, stretch, wq, wv, bias, after)

    far_own, far_other = attend_side(1, own.reshape(2, nz * shard_rows, padded))
    far = merge_pair(far_own, lax.ppermute(far_other, "c", swap(nc)))
    crossed = lax.ppermute(far, "yh", swap(ny))
    near_own, near_other = attend_side(0, far)
    sends = merge_send(near_own, lax.ppermute(near_other, "c", swap(nc)), crossed)
    parts = lax.all_to_all(sends, ("z", "x", "yl"), 0, 0, tiled=True)
    outs = finish(parts.reshape(nz, groups * 2 * rows, padded), groups, rows)
    return tuple(o.transpose(1, 0, 2).reshape(rows, model) for o in outs)


def solution(mesh):
    axes = ("z", "yh", "c", "x", "yl")
    torus = Mesh(mesh.devices.reshape(8, 2, 2, 4, 2), axes)
    tokens = P(axes, None)
    cache = P(axes[:3], axes[3:])
    return jax.shard_map(
        local,
        mesh=torus,
        in_specs=(tokens,) * 4 + (cache,) * 2 + (P(),) * 5,
        out_specs=(tokens, tokens),
        check_vma=False,
    )
```

profile of v0, /device:TPU:16, one launch (start us, length us, event | category | flops | bytes accessed | tf_op | source)
XLA Modules:
  0.0 123.0 jit_solution(7764439557654871905)
XLA Ops:
  0.6 2.1 %prepare.1 = bf16[8,2,3328]{2,1,0:T(2,128)(2,1)} custom-call(bf16[2,8192]{1,0:T(2,128)(2,1)} %x_ref.1, bf16[8,2,1024]{2,1,0:T(2,128)(2,1)} %bitcast.33, bf16[8,2,1024]{2,1,0:T(2,128)(2,1)} %bitcast.34, bf16[8,2,1024]{2,1,0:T(2,128)(2,1)} %bitcast.35, bf16[16,8192]{1,0:T(8,128)(2,1)} %bitcast.30, bf16[16,8192]{1,0:T(8,128)(2,1)} %bitcast.31), custom_call_target="tpu_custom_call" | custom-call | tf_op jit(solution)/shard_map/prepare/pallas_call | solution.py:48
  2.7 11.3 %all_to_all.15 = bf16[8,2,3328]{2,1,0:T(2,128)(2,1)S(1)} all-to-all(bf16[8,2,3328]{2,1,0:T(2,128)(2,1)} %prepare.1), channel_id=1, replica_groups=mesh['z'=8,'yh'=2,'c'=2,'x'=4,'yl'=2] {'x','yl'}, dimensions={0} | all-to-all | bytes 212992 | tf_op jit(solution)/shard_map/all_to_all | solution.py:336
  14.1 0.7 collective-permute-start
  14.9 4.8 %collective-permute-done.far_ref = bf16[16,1152]{1,0:T(8,128)(2,1)S(1)} collective-permute-done((bf16[16,1152]{1,0:T(8,128)(2,1)S(1)}, bf16[16,1152]{1,0:T(8,128)(2,1)S(1)}, u32[]{:S(2)}, u32[]{:S(2)}) %collective-permute-start) | collective-permute-done | bytes 36896 | tf_op jit(solution)/shard_map/ppermute | solution.py:337
  19.7 0.6 copy-done.4
  20.3 1.8 %fan.1 = bf16[8,32,1152]{2,1,0:T(8,128)(2,1)} custom-call(bf16[16,3328]{1,0:T(8,128)(2,1)} %copy-done.1, bf16[16,1152]{1,0:T(8,128)(2,1)} %copy-done.4), custom_call_target="tpu_custom_call" | custom-call | tf_op jit(solution)/shard_map/fan/pallas_call | solution.py:67
  22.1 8.5 %all-to-all-start.1 = ((bf16[8,32,1152]{2,1,0:T(8,128)(2,1)}), bf16[8,32,1152]{2,1,0:T(8,128)(2,1)S(1)}, u32[]{:S(2)}, u32[]{:S(2)}) async-start(bf16[8,32,1152]{2,1,0:T(8,128)(2,1)} %fan.1), calls=%async_computation.1 | async-start | bytes 1179648 | tf_op jit(solution)/shard_map/all_to_all | solution.py:338
  30.6 16.3 %all-to-all-done.1 = bf16[8,32,1152]{2,1,0:T(8,128)(2,1)S(1)} async-done(((bf16[8,32,1152]{2,1,0:T(8,128)(2,1)}), bf16[8,32,1152]{2,1,0:T(8,128)(2,1)S(1)}, u32[]{:S(2)}, u32[]{:S(2)}) %all-to-all-start.1) | async-done | bytes 589856 | tf_op jit(solution)/shard_map/all_to_all | solution.py:338
  46.9 0.1 pad_add_fusion.1.where_ref
  46.9 0.1 eq.23
  47.1 0.1 le.36
  47.2 0.1 iota.36
  47.3 0.1 eq.25
  47.3 0.8 constant_dynamic-slice_fusion
  48.2 0.2 and_select_fusion.bias_ref
  48.4 0.5 collective-permute-done.1
  48.9 0.9 copy-done.2
  49.8 12.7 %attend.2 = (bf16[2,128,1152]{2,1,0:T(8,128)(2,1)S(1)}, bf16[2,128,1152]{2,1,0:T(8,128)(2,1)S(1)}) custom-call(s32[3]{0:T(128)S(1)} %pad_add_fusion.1.where_ref, bf16[8,2,16,1152]{3,2,1,0:T(8,128)(2,1)S(1)} %bitcast.25, bf16[8,2,16,1152]{3,2,1,0:T(8,128)(2,1)S(1)} %bitcast.28, bf16[1536,1024]{1,0:T(8,128)(2,1)} %keys_hbm.3, bf16[1536,1024]{1,0:T(8,128)(2,1)} %values_hbm.3, ...), custom_call_target="tpu_custom_call" | custom-call | flops 3221225472 | bytes 6291456 | tf_op jit(solution)/shard_map/attend/pallas_call | solution.py:203
  62.5 0.4 collective-permute-start.2
  62.9 0.1 pad_add_fusion.where_ref
  62.9 1.8 %collective-permute-done.2.b_ref = bf16[2,128,1152]{2,1,0:T(8,128)(2,1)S(1)} collective-permute-done((bf16[2,128,1152]{2,1,0:T(8,128)(2,1)S(1)}, bf16[2,128,1152]{2,1,0:T(8,128)(2,1)S(1)}, u32[]{:S(2)}, u32[]{:S(2)}) %collective-permute-start.2) | collective-permute-done | bytes 589856 | tf_op jit(solution)/shard_map/ppermute | solution.py:360
  64.7 1.1 merge_pair.1.after_ref
  65.9 0.8 copy-done
  66.7 12.8 %attend.3 = (bf16[2,128,1152]{2,1,0:T(8,128)(2,1)S(1)}, bf16[2,128,1152]{2,1,0:T(8,128)(2,1)S(1)}) custom-call(s32[3]{0:T(128)S(1)} %pad_add_fusion.where_ref, bf16[8,2,16,1152]{3,2,1,0:T(8,128)(2,1)S(1)} %bitcast.27, bf16[8,2,16,1152]{3,2,1,0:T(8,128)(2,1)S(1)} %bitcast.29, bf16[1536,1024]{1,0:T(8,128)(2,1)} %keys_hbm.3, bf16[1536,1024]{1,0:T(8,128)(2,1)} %values_hbm.3, ...), custom_call_target="tpu_custom_call" | custom-call | flops 3221225472 | bytes 6291456 | tf_op jit(solution)/shard_map/attend/pallas_call | solution.py:203
  79.5 0.2 collective-permute-start.3
  79.8 0.6 collective-permute-start.4
  80.4 1.2 collective-permute-done.3.b_ref
  81.6 15.5 %collective-permute-done.4.c_ref = bf16[2,128,1152]{2,1,0:T(8,128)(2,1)S(1)} collective-permute-done((bf16[2,128,1152]{2,1,0:T(8,128)(2,1)}, bf16[2,128,1152]{2,1,0:T(8,128)(2,1)S(1)}, u32[]{:S(2)}, u32[]{:S(2)}) %collective-permute-start.4) | collective-permute-done | bytes 589856 | tf_op jit(solution)/shard_map/ppermute | solution.py:361
  97.1 1.6 %merge_send.1 = bf16[64,2,2,1152]{3,2,1,0:T(2,128)(2,1)S(1)} custom-call(bf16[2,128,1152]{2,1,0:T(8,128)(2,1)S(1)} %get-tuple-element.10.a_ref, bf16[2,128,1152]{2,1,0:T(8,128)(2,1)S(1)} %collective-permute-done.3.b_ref, bf16[2,128,1152]{2,1,0:T(8,128)(2,1)S(1)} %collective-permute-done.4.c_ref), custom_call_target="tpu_custom_call" | custom-call | flops 3538944 | bytes 2359296 | tf_op jit(solution)/shard_map/merge_send/pallas_call | solution.py:273
  98.7 23.0 %all_to_all.16 = bf16[64,2,2,1152]{3,2,1,0:T(2,128)(2,1)S(1)} all-to-all(bf16[64,2,2,1152]{3,2,1,0:T(2,128)(2,1)S(1)} %merge_send.1), channel_id=1, replica_groups=mesh['z'=8,'yh'=2,'c'=2,'x'=4,'yl'=2] {'z','x','yl'}, dimensions={0} | all-to-all | bytes 1179648 | tf_op jit(solution)/shard_map/all_to_all | solution.py:364
  121.7 0.2 reshape.80.x_ref
  121.9 1.1 finish.1
  (18 shorter events, 0.2 us)
Async XLA Ops:
  0.6 46.3 %copy-start.5 = (s32[512]{0:T(512)S(1)}, s32[512]{0:T(512)}, u32[]{:S(2)}) copy-start(s32[512]{0:T(512)} %param.21) | copy-start | bytes 6148
  14.1 5.6 %copy-start.1 = (bf16[16,3328]{1,0:T(8,128)(2,1)}, bf16[16,3328]{1,0:T(8,128)(2,1)S(1)}, u32[]{:S(2)}) copy-start(bf16[16,3328]{1,0:T(8,128)(2,1)S(1)} %reshape.77.near_ref.stretch_ref) | copy-start | bytes 319492
  14.1 5.5 %collective-permute-start = (bf16[16,1152]{1,0:T(8,128)(2,1)S(1)}, bf16[16,1152]{1,0:T(8,128)(2,1)S(1)}, u32[]{:S(2)}, u32[]{:S(2)}) collective-permute-start(bf16[16,1152]{1,0:T(8,128)(2,1)S(1)} %slice.4), channel_id=1, source_target_pairs={{0,16},{16,0},{1,17},{17,1},{2,18},{18,2},{3,19},{19,3},{4,20},{20... | collective-permute-start | bytes 110600 | tf_op jit(solution)/shard_map/ppermute | solution.py:337
  19.7 0.6 copy-start.4
  22.1 24.8 %all-to-all-start.1 = ((bf16[8,32,1152]{2,1,0:T(8,128)(2,1)}), bf16[8,32,1152]{2,1,0:T(8,128)(2,1)S(1)}, u32[]{:S(2)}, u32[]{:S(2)}) async-start(bf16[8,32,1152]{2,1,0:T(8,128)(2,1)} %fan.1), calls=%async_computation.1 | async-start | bytes 1179648 | tf_op jit(solution)/shard_map/all_to_all | solution.py:338
  46.9 2.0 %collective-permute-start.1 = (bf16[8,32,1152]{2,1,0:T(8,128)(2,1)S(1)}, bf16[8,32,1152]{2,1,0:T(8,128)(2,1)S(1)}, u32[]{:S(2)}, u32[]{:S(2)}) collective-permute-start(bf16[8,32,1152]{2,1,0:T(8,128)(2,1)S(1)} %all-to-all-done.1), channel_id=1, source_target_pairs={{0,8},{8,0},{1,9},{9,1},{2,10},{10,2},{3,11},{11,3},{4,12},{12,4},... | collective-permute-start | bytes 1769480 | tf_op jit(solution)/shard_map/ppermute | solution.py:339
  48.9 0.9 copy-start.2
  49.8 16.9 %copy-start.3 = (bf16[16,3328]{1,0:T(8,128)(2,1)S(1)}, bf16[16,3328]{1,0:T(8,128)(2,1)}, u32[]{:S(2)}) copy-start(bf16[16,3328]{1,0:T(8,128)(2,1)} %copy-done.1) | copy-start | bytes 319492
  62.5 2.3 %collective-permute-start.2 = (bf16[2,128,1152]{2,1,0:T(8,128)(2,1)S(1)}, bf16[2,128,1152]{2,1,0:T(8,128)(2,1)S(1)}, u32[]{:S(2)}, u32[]{:S(2)}) collective-permute-start(bf16[2,128,1152]{2,1,0:T(8,128)(2,1)S(1)} %get-tuple-element.9), channel_id=1, source_target_pairs={{0,8},{8,0},{1,9},{9,1},{2,10},{10,2},{3,11},{11,3},{4,12},{12,4},... | collective-permute-start | bytes 1769480 | tf_op jit(solution)/shard_map/ppermute | solution.py:360
  65.9 0.8 copy-start
  79.5 2.1 %collective-permute-start.3 = (bf16[2,128,1152]{2,1,0:T(8,128)(2,1)S(1)}, bf16[2,128,1152]{2,1,0:T(8,128)(2,1)S(1)}, u32[]{:S(2)}, u32[]{:S(2)}) collective-permute-start(bf16[2,128,1152]{2,1,0:T(8,128)(2,1)S(1)} %get-tuple-element.11), channel_id=1, source_target_pairs={{0,8},{8,0},{1,9},{9,1},{2,10},{10,2},{3,11},{11,3},{4,12},{12,4},... | collective-permute-start | bytes 1769480 | tf_op jit(solution)/shard_map/ppermute | solution.py:363
  79.8 17.3 %collective-permute-start.4 = (bf16[2,128,1152]{2,1,0:T(8,128)(2,1)}, bf16[2,128,1152]{2,1,0:T(8,128)(2,1)S(1)}, u32[]{:S(2)}, u32[]{:S(2)}) collective-permute-start(bf16[2,128,1152]{2,1,0:T(8,128)(2,1)} %copy-done), channel_id=1, source_target_pairs={{0,16},{16,0},{1,17},{17,1},{2,18},{18,2},{3,19},{19,3},{4,20},{20... | collective-permute-start | bytes 1769480 | tf_op jit(solution)/shard_map/ppermute | solution.py:361
where the time goes:
time: 123 us
  waiting for transfers between devices  40.1 us (33%)
  blocking collectives  34.3 us (28%)
  Pallas kernels  33.2 us (27%)
  starting transfers between devices  10.5 us (9%)
  local copies, waits for them, and re-layouts  3.8 us (3%)
    pallas_call x2, Pallas kernels, attend(): pl.pallas_call(attend_kernel, in_specs=[pl.BlockSpec(memory_space=pltpu.S...  25.5 us
    all_to_all x1, blocking collectives, local(): parts = lax.all_to_all(sends, ('z', 'x', 'yl'), 0, 0, tiled=True)  23 us
    all_to_all x1, waiting for transfers between devices, local(): own = lax.all_to_all(fan(stretch, far_rows, nz), 'z', 0, 0, tiled=True)  16.3 us
    ppermute x1, waiting for transfers between devices, local(): crossed = lax.ppermute(far, 'yh', swap(ny))  15.5 us
    all_to_all x1, blocking collectives, local(): lax.all_to_all(sent, ('x', 'yl'), 0, 0, tiled=True)  11.3 us
    all_to_all x1, starting transfers between devices, local(): own = lax.all_to_all(fan(stretch, far_rows, nz), 'z', 0, 0, tiled=True)  8.47 us
    ppermute x1, waiting for transfers between devices, local(): far_rows = lax.ppermute(stretch[:, :padded], 'yh', swap(ny))  4.83 us
  transfers between devices with their start and end apart: 6, of which 6 were waited for; matrix products, arithmetic and copies ran while one was open for 1% of the time, Pallas kernels for 0%

commit v1 on v0

--- a/solution.py
+++ b/solution.py
@@ -39,36 +39,37 @@
     for g in range(q_ref.shape[0]):
         at = 0
         for piece in (q_ref[g], fq, k_ref[g], v_ref[g], fv):
-            out_ref[g, :, at : at + piece.shape[1]] = piece
+            for half in range(out_ref.shape[0]):
+                out_ref[half, g, :, at : at + piece.shape[1]] = piece
             at += piece.shape[1]
 
 
-def prepare(x, q, k, v, wq, wv):
+def prepare(x, q, k, v, wq, wv, halves):
     groups, rows, width = q.shape
     return pl.pallas_call(
         prepare_kernel,
-        out_shape=jax.ShapeDtypeStruct((groups, rows, 3 * width + 256), BF16),
+        out_shape=jax.ShapeDtypeStruct((halves, groups, rows, 3 * width + 256), BF16),
         scratch_shapes=[pltpu.VMEM((2, rows, 128), F32)],
         name="prepare",
     )(x, q, k, v, wq, wv)
 
 
-def fan_kernel(near_ref, far_ref, out_ref):
-    rows, padded = far_ref.shape
-    near = near_ref[:, :padded]
-    far = far_ref[...]
+def fan_kernel(rows_ref, out_ref):
+    rows = rows_ref[...]
     for z in range(out_ref.shape[0]):
-        out_ref[z, :rows] = near
-        out_ref[z, rows:] = far
-
-
-def fan(near, far, parts):
-    rows, padded = far.shape
+        out_ref[z] = rows
+
+
+def fan(rows, parts, padded):
+    count = rows.shape[0]
     return pl.pallas_call(
         fan_kernel,
-        out_shape=jax.ShapeDtypeStruct((parts, 2 * rows, padded), BF16),
+        grid=(1,),
+        in_specs=[pl.BlockSpec((count, padded), lambda i: (0, 0))],
+        out_specs=pl.BlockSpec((parts, count, padded), lambda i: (0, 0, 0)),
+        out_shape=jax.ShapeDtypeStruct((parts, count, padded), BF16),
         name="fan",
-    )(near, far)
+    )(rows)
 
 
 def pack_lse(lse, lane):
@@ -119,7 +120,8 @@
         return ref[:, side, :, at : at + size].reshape(n, size)
 
     factors = jnp.concatenate([tokens(own_ref, width, HD), tokens(other_ref, width, HD)], 0)[:, :rank]
-    value_factors = stretch_ref[:, factors_at : factors_at + rank]
+    home = where_ref[3]
+    value_factors = stretch_ref[home, :, factors_at : factors_at + rank]
 
     def begin(h):
         at = h * HD
@@ -128,7 +130,7 @@
             base.astype(F32) + jnp.dot(factors, wq_ref[:, at : at + HD], preferred_element_type=F32)
         ).astype(BF16)
         q = jnp.concatenate([adapted, base], 0)
-        near = lax.dot_general(q, stretch_ref[:, keys_at + at : keys_at + at + HD], LAST_DIMS, preferred_element_type=F32) + bias
+        near = lax.dot_general(q, stretch_ref[home, :, keys_at + at : keys_at + at + HD], LAST_DIMS, preferred_element_type=F32) + bias
         max_refs[h % 2][...] = jnp.broadcast_to(jnp.max(near, -1, keepdims=True), (rows, 128))
         return q, near
 
@@ -154,11 +156,10 @@
         if h + 1 < heads:
             q, near_next = begin(h + 1)
         m = jnp.max(max_refs[h % 2][...], -1, keepdims=True)
-        shift = m * (SCALE * LOG2E)
-        near_probs = jnp.exp2(near * (SCALE * LOG2E) - shift)
+        near_probs = jnp.exp2((near - m) * (SCALE * LOG2E))
         near_total = jnp.sum(near_probs, -1, keepdims=True)
         near_probs = near_probs.astype(BF16)
-        base_values = stretch_ref[:, values_at + at : values_at + at + HD]
+        base_values = stretch_ref[home, :, values_at + at : values_at + at + HD]
         adapted_values = (
             base_values.astype(F32) + jnp.dot(value_factors, wv_ref[:, at : at + HD], preferred_element_type=F32)
         ).astype(BF16)
@@ -168,7 +169,7 @@
         for j in range(0, kn, KEY_CHUNK):
             if h + 1 < heads:
                 score(h + 1, q, j)
-            p = jnp.exp2(scores_refs[h % 2][:, j : j + KEY_CHUNK] * (SCALE * LOG2E) - shift)
+            p = jnp.exp2((scores_refs[h % 2][:, j : j + KEY_CHUNK] - m) * (SCALE * LOG2E))
             total = l_ref[...]
             for c in range(0, KEY_CHUNK, 128):
                 total += p[:, c : c + 128]
@@ -332,10 +333,11 @@
         by_group(response_values),
         query_down_weight.T,
         value_down_weight.T,
-    )
-    stretch = lax.all_to_all(sent, ("x", "yl"), 0, 0, tiled=True).reshape(shard_rows, 3 * width + 256)
-    far_rows = lax.ppermute(stretch[:, :padded], "yh", swap(ny))
-    own = lax.all_to_all(fan(stretch, far_rows, nz), "z", 0, 0, tiled=True)
+        ny,
+    ).reshape(ny * groups, rows, 3 * width + 256)
+    rows_in = lax.all_to_all(sent, ("yh", "x", "yl"), 0, 0, tiled=True).reshape(ny * shard_rows, 3 * width + 256)
+    stretch = rows_in.reshape(ny, shard_rows, 3 * width + 256)
+    own = lax.all_to_all(fan(rows_in, nz, padded), "z", 0, 0, tiled=True)
     other = lax.ppermute(own, "c", swap(nc))
     own = own.reshape(nz, ny, shard_rows, padded)
     other = other.reshape(nz, ny, shard_rows, padded)
@@ -352,8 +354,8 @@
     bias = bias.reshape(ny * nc, nz * shard_rows, shard_rows)
 
     def attend_side(far, after):
-        half = 2 * (side ^ far)
-        where = jnp.stack([jnp.int32(far), half + core, half + 1 - core]).astype(jnp.int32)
+        to = side ^ far
+        where = jnp.stack([to, 2 * to + core, 2 * to + 1 - core, side]).astype(jnp.int32)
         return attend(where, own, other, prompt_keys, prompt_values, stretch, wq, wv, bias, after)
 
     far_own, far_other = attend_side(1, own.reshape(2, nz * shard_rows, padded))

time: 123 us -> 121 us (0.984); the launches traced: 123 us -> 119 us
  waiting for transfers between devices: 40.1 us -> 35.3 us
  blocking collectives: 34.3 us -> 36.6 us
    ppermute x1 -> x0, waiting for transfers between devices: 4.83 us -> none  [local(): far_rows = lax.ppermute(stretch[:, :padded], 'yh', swap(ny))]
    all_to_all x1, blocking collectives: 11.3 us -> 13.6 us  [local(): lax.all_to_all(sent, ('yh', 'x', 'yl'), 0, 0, tiled=True)]
    unnamed x12 -> x4, local copies, waits for them, and re-layouts: 2.33 us -> 0.8 us
    all_to_all x1, waiting for transfers between devices: 16.3 us -> 17.7 us  [local(): own = lax.all_to_all(fan(rows_in, nz, padded), 'z', 0, 0, tiled=True)]
    ppermute x1, starting transfers between devices: 0.64 us -> 1.92 us  [local(): crossed = lax.ppermute(far, 'yh', swap(ny))]
  transfers between devices with their start and end apart: 6 -> 5, of which waited for: 6 -> 4; matrix products, arithmetic and copies ran while one was open for 1% -> 1% of each run, Pallas kernels for 0% -> 0%
where the time goes in v1:
time: 121 us; the launch traced here: 119 us
  blocking collectives  36.6 us (30%)
  waiting for transfers between devices  35.3 us (29%)
  Pallas kernels  32 us (26%)
  starting transfers between devices  11.2 us (9%)
  local copies, waits for them, and re-layouts  3.06 us (3%)
    pallas_call x2, Pallas kernels, attend(): pl.pallas_call(attend_kernel, in_specs=[pl.BlockSpec(memory_space=pltpu.S...  24.3 us
    all_to_all x1, blocking collectives, local(): parts = lax.all_to_all(sends, ('z', 'x', 'yl'), 0, 0, tiled=True)  23 us
    all_to_all x1, waiting for transfers between devices, local(): own = lax.all_to_all(fan(rows_in, nz, padded), 'z', 0, 0, tiled=True)  17.7 us
    ppermute x1, waiting for transfers between devices, local(): crossed = lax.ppermute(far, 'yh', swap(ny))  15.4 us
    all_to_all x1, blocking collectives, local(): lax.all_to_all(sent, ('yh', 'x', 'yl'), 0, 0, tiled=True)  13.6 us
    all_to_all x1, starting transfers between devices, local(): own = lax.all_to_all(fan(rows_in, nz, padded), 'z', 0, 0, tiled=True)  8.47 us
  transfers between devices with their start and end apart: 5, of which 4 were waited for; matrix products, arithmetic and copies ran while one was open for 1% of the time, Pallas kernels for 0%

profile of v1, /device:TPU:16, one launch (start us, length us, event | category | flops | bytes accessed | tf_op | source)
XLA Modules:
  0.0 119.3 jit_solution(5080930696943029327)
XLA Ops:
  0.6 2.1 %prepare.1 = bf16[2,8,2,3328]{3,2,1,0:T(2,128)(2,1)} custom-call(bf16[2,8192]{1,0:T(2,128)(2,1)} %x_ref.1, bf16[8,2,1024]{2,1,0:T(2,128)(2,1)} %bitcast.37, bf16[8,2,1024]{2,1,0:T(2,128)(2,1)} %bitcast.38, bf16[8,2,1024]{2,1,0:T(2,128)(2,1)} %bitcast.39, bf16[16,8192]{1,0:T(8,128)(2,1)} %bitcast.34, bf16[16,8192]{1,0:T(8,128)(2,1)} %bitcast.35), custom_call_target="tpu_custom_call" | custom-call | tf_op jit(solution)/shard_map/prepare/pallas_call | solution.py:49
  2.8 13.6 %all_to_all.15 = bf16[16,2,3328]{2,1,0:T(2,128)(2,1)S(1)} all-to-all(bf16[16,2,3328]{2,1,0:T(2,128)(2,1)} %bitcast.33), channel_id=1, replica_groups=mesh['z'=8,'yh'=2,'c'=2,'x'=4,'yl'=2] {'yh','x','yl'}, dimensions={0} | all-to-all | bytes 425984 | tf_op jit(solution)/shard_map/all_to_all | solution.py:338
  16.4 0.8 reshape.81.rows_ref
  17.1 1.7 %fan.1 = bf16[8,32,1152]{2,1,0:T(8,128)(2,1)} custom-call(bf16[32,3328]{1,0:T(8,128)(2,1)} %reshape.81.rows_ref), custom_call_target="tpu_custom_call" | custom-call | tf_op jit(solution)/shard_map/fan/pallas_call | solution.py:65
  18.8 8.5 %all-to-all-start.1 = ((bf16[8,32,1152]{2,1,0:T(8,128)(2,1)}), bf16[8,32,1152]{2,1,0:T(8,128)(2,1)S(1)}, u32[]{:S(2)}, u32[]{:S(2)}) async-start(bf16[8,32,1152]{2,1,0:T(8,128)(2,1)} %fan.1), calls=%async_computation.1 | async-start | bytes 1179648 | tf_op jit(solution)/shard_map/all_to_all | solution.py:340
  27.3 17.7 %all-to-all-done.1 = bf16[8,32,1152]{2,1,0:T(8,128)(2,1)S(1)} async-done(((bf16[8,32,1152]{2,1,0:T(8,128)(2,1)}), bf16[8,32,1152]{2,1,0:T(8,128)(2,1)S(1)}, u32[]{:S(2)}, u32[]{:S(2)}) %all-to-all-start.1) | async-done | bytes 589856 | tf_op jit(solution)/shard_map/all_to_all | solution.py:340
  45.0 0.0 collective-permute-start
  45.0 0.1 add_add_fusion.2.where_ref
  45.1 0.1 eq.23
  45.2 0.1 dynamic_slice.11
  45.3 0.1 le.36
  45.4 0.1 iota.36
  45.4 0.1 eq.25
  45.5 0.8 constant_dynamic-slice_fusion
  46.3 0.2 and_select_fusion.bias_ref
  46.5 0.1 reshape_reshape.6.stretch_ref
  46.6 0.4 collective-permute-done
  47.0 12.1 %attend.2 = (bf16[2,128,1152]{2,1,0:T(8,128)(2,1)S(1)}, bf16[2,128,1152]{2,1,0:T(8,128)(2,1)S(1)}) custom-call(s32[4]{0:T(128)S(1)} %add_add_fusion.2.where_ref, bf16[8,2,16,1152]{3,2,1,0:T(8,128)(2,1)S(1)} %bitcast.28, bf16[8,2,16,1152]{3,2,1,0:T(8,128)(2,1)S(1)} %bitcast.31, bf16[1536,1024]{1,0:T(8,128)(2,1)} %keys_hbm.3, bf16[1536,1024]{1,0:T(8,128)(2,1)} %values_hbm.3, ...), custom_call_target="tpu_custom_call" | custom-call | flops 3221225472 | bytes 6291456 | tf_op jit(solution)/shard_map/attend/pallas_call | solution.py:204
  59.2 0.4 collective-permute-start.1
  59.5 0.1 add_add_fusion.1.where_ref
  59.6 1.8 %collective-permute-done.1.b_ref = bf16[2,128,1152]{2,1,0:T(8,128)(2,1)S(1)} collective-permute-done((bf16[2,128,1152]{2,1,0:T(8,128)(2,1)S(1)}, bf16[2,128,1152]{2,1,0:T(8,128)(2,1)S(1)}, u32[]{:S(2)}, u32[]{:S(2)}) %collective-permute-start.1) | collective-permute-done | bytes 589856 | tf_op jit(solution)/shard_map/ppermute | solution.py:362
  61.4 1.1 merge_pair.1.after_ref
  62.6 0.8 copy-done
  63.4 12.2 %attend.3 = (bf16[2,128,1152]{2,1,0:T(8,128)(2,1)S(1)}, bf16[2,128,1152]{2,1,0:T(8,128)(2,1)S(1)}) custom-call(s32[4]{0:T(128)S(1)} %add_add_fusion.1.where_ref, bf16[8,2,16,1152]{3,2,1,0:T(8,128)(2,1)S(1)} %bitcast.30, bf16[8,2,16,1152]{3,2,1,0:T(8,128)(2,1)S(1)} %bitcast.32, bf16[1536,1024]{1,0:T(8,128)(2,1)} %keys_hbm.3, bf16[1536,1024]{1,0:T(8,128)(2,1)} %values_hbm.3, ...), custom_call_target="tpu_custom_call" | custom-call | flops 3221225472 | bytes 6291456 | tf_op jit(solution)/shard_map/attend/pallas_call | solution.py:204
  75.6 0.4 collective-permute-start.2
  76.0 1.9 %collective-permute-start.3 = (bf16[2,128,1152]{2,1,0:T(8,128)(2,1)}, bf16[2,128,1152]{2,1,0:T(8,128)(2,1)S(1)}, u32[]{:S(2)}, u32[]{:S(2)}) collective-permute-start(bf16[2,128,1152]{2,1,0:T(8,128)(2,1)} %copy-done), channel_id=1, source_target_pairs={{0,16},{16,0},{1,17},{17,1},{2,18},{18,2},{3,19},{19,3},{4,20},{20... | collective-permute-start | bytes 1769480 | tf_op jit(solution)/shard_map/ppermute | solution.py:363
  78.0 0.0 collective-permute-done.2.b_ref
  78.0 15.4 %collective-permute-done.3.c_ref = bf16[2,128,1152]{2,1,0:T(8,128)(2,1)S(1)} collective-permute-done((bf16[2,128,1152]{2,1,0:T(8,128)(2,1)}, bf16[2,128,1152]{2,1,0:T(8,128)(2,1)S(1)}, u32[]{:S(2)}, u32[]{:S(2)}) %collective-permute-start.3) | collective-permute-done | bytes 589856 | tf_op jit(solution)/shard_map/ppermute | solution.py:363
  93.4 1.6 %merge_send.1 = bf16[64,2,2,1152]{3,2,1,0:T(2,128)(2,1)S(1)} custom-call(bf16[2,128,1152]{2,1,0:T(8,128)(2,1)S(1)} %get-tuple-element.10.a_ref, bf16[2,128,1152]{2,1,0:T(8,128)(2,1)S(1)} %collective-permute-done.2.b_ref, bf16[2,128,1152]{2,1,0:T(8,128)(2,1)S(1)} %collective-permute-done.3.c_ref), custom_call_target="tpu_custom_call" | custom-call | flops 3538944 | bytes 2359296 | tf_op jit(solution)/shard_map/merge_send/pallas_call | solution.py:274
  95.0 23.0 %all_to_all.16 = bf16[64,2,2,1152]{3,2,1,0:T(2,128)(2,1)S(1)} all-to-all(bf16[64,2,2,1152]{3,2,1,0:T(2,128)(2,1)S(1)} %merge_send.1), channel_id=1, replica_groups=mesh['z'=8,'yh'=2,'c'=2,'x'=4,'yl'=2] {'z','x','yl'}, dimensions={0} | all-to-all | bytes 1179648 | tf_op jit(solution)/shard_map/all_to_all | solution.py:366
  117.9 0.2 reshape.84.x_ref
  118.2 1.1 finish.1
  (8 shorter events, 0.0 us)
Async XLA Ops:
  0.6 44.5 %copy-start.1 = (s32[512]{0:T(512)S(1)}, s32[512]{0:T(512)}, u32[]{:S(2)}) copy-start(s32[512]{0:T(512)} %param.21) | copy-start | bytes 6148
  18.8 26.2 %all-to-all-start.1 = ((bf16[8,32,1152]{2,1,0:T(8,128)(2,1)}), bf16[8,32,1152]{2,1,0:T(8,128)(2,1)S(1)}, u32[]{:S(2)}, u32[]{:S(2)}) async-start(bf16[8,32,1152]{2,1,0:T(8,128)(2,1)} %fan.1), calls=%async_computation.1 | async-start | bytes 1179648 | tf_op jit(solution)/shard_map/all_to_all | solution.py:340
  45.0 2.0 %collective-permute-start = (bf16[8,32,1152]{2,1,0:T(8,128)(2,1)S(1)}, bf16[8,32,1152]{2,1,0:T(8,128)(2,1)S(1)}, u32[]{:S(2)}, u32[]{:S(2)}) collective-permute-start(bf16[8,32,1152]{2,1,0:T(8,128)(2,1)S(1)} %all-to-all-done.1), channel_id=1, source_target_pairs={{0,8},{8,0},{1,9},{9,1},{2,10},{10,2},{3,11},{11,3},{4,12},{12,4},... | collective-permute-start | bytes 1769480 | tf_op jit(solution)/shard_map/ppermute | solution.py:341
  59.2 2.3 %collective-permute-start.1 = (bf16[2,128,1152]{2,1,0:T(8,128)(2,1)S(1)}, bf16[2,128,1152]{2,1,0:T(8,128)(2,1)S(1)}, u32[]{:S(2)}, u32[]{:S(2)}) collective-permute-start(bf16[2,128,1152]{2,1,0:T(8,128)(2,1)S(1)} %get-tuple-element.9), channel_id=1, source_target_pairs={{0,8},{8,0},{1,9},{9,1},{2,10},{10,2},{3,11},{11,3},{4,12},{12,4},... | collective-permute-start | bytes 1769480 | tf_op jit(solution)/shard_map/ppermute | solution.py:362
  62.6 0.8 copy-start
  75.6 2.4 %collective-permute-start.2 = (bf16[2,128,1152]{2,1,0:T(8,128)(2,1)S(1)}, bf16[2,128,1152]{2,1,0:T(8,128)(2,1)S(1)}, u32[]{:S(2)}, u32[]{:S(2)}) collective-permute-start(bf16[2,128,1152]{2,1,0:T(8,128)(2,1)S(1)} %get-tuple-element.11), channel_id=1, source_target_pairs={{0,8},{8,0},{1,9},{9,1},{2,10},{10,2},{3,11},{11,3},{4,12},{12,4},... | collective-permute-start | bytes 1769480 | tf_op jit(solution)/shard_map/ppermute | solution.py:365
  76.0 17.3 %collective-permute-start.3 = (bf16[2,128,1152]{2,1,0:T(8,128)(2,1)}, bf16[2,128,1152]{2,1,0:T(8,128)(2,1)S(1)}, u32[]{:S(2)}, u32[]{:S(2)}) collective-permute-start(bf16[2,128,1152]{2,1,0:T(8,128)(2,1)} %copy-done), channel_id=1, source_target_pairs={{0,16},{16,0},{1,17},{17,1},{2,18},{18,2},{3,19},{19,3},{4,20},{20... | collective-permute-start | bytes 1769480 | tf_op jit(solution)/shard_map/ppermute | solution.py:363
